TPU v7x, 32 devices: a whole 2x2x4 slice. The times are simulated.
32 devices in a mesh: member: 8 (over z, x), space: 4 (over y, core).
Axes of the slice: x: 2, y: 2, z: 4, core: 2. Of those that a mesh axis runs over, the one named last changes fastest.
Arguments:
- states: float32 [1024, 24576], P('member', 'space'), may hold values from -6 to 6
- obs_values: float32 [2, 2048], replicated, may hold values from -6 to 6
- obs_weights: float32 [2, 2048], replicated, may hold values from 0.2 to 2
- obs_cell: int32 [2, 4, 4], P(None, 'space'), may hold values from 0 to 47
- op_select: int32 [2, 4, 4], P(None, 'space'), may hold values from 0 to 7
- op_table: float32 [8, 128, 128], replicated, may hold values from -0.5 to 0.5
- loc_obs: int32 [2, 4, 48, 8], P(None, 'space', 'member'), may hold values from 0 to 11
- loc_tile: int32 [2, 4, 48, 8], P(None, 'space', 'member'), may hold values from 0 to 7
- loc_tiles: float32 [8, 128, 128], replicated, may hold values from 0 to 1
Outputs:
- analysis: float32 [1024, 24576], P('member', 'space')
All inputs are finite; a program needn't handle non-finite values.
Results may differ from a plain program's by a relative error of at most 0.00012.
Values sent between devices are 32-bit elements; how exact they have to be, the bound alone decides.
A program may use at most 128 MiB of HBM per device.

v0:
```python
import jax
import jax.numpy as jnp
from jax import lax
from jax.sharding import PartitionSpec as P

K = 1024
BLK = 128
CB_DEV = 6
OB = 4


def with_halo(cells, sides, width):
    for axis, dim in sides:
        count = lax.axis_size(axis)
        head = lax.slice_in_dim(cells, 0, width, axis=dim)
        tail = lax.slice_in_dim(cells, cells.shape[dim] - width, cells.shape[dim], axis=dim)
        cells = jnp.concatenate(
            [
                lax.ppermute(tail, axis, [(i, (i + 1) % count) for i in range(count)]),
                cells,
                lax.ppermute(head, axis, [((i + 1) % count, i) for i in range(count)]),
            ],
            axis=dim,
        )
    return cells


def window_values(flat_row):
    space_n = lax.axis_size("space")
    slab_index = lax.axis_index("space")
    by_slab = flat_row.reshape(space_n, OB * BLK)
    slab_pick = (slab_index - 1 + jnp.arange(3, dtype=jnp.int32)) % space_n
    return by_slab[slab_pick].reshape(3 * OB * BLK)


def window(observed):
    return with_halo(observed, (("space", 1),), OB * BLK)


def prepare(window_obs, obs_values, obs_weights, batch_no):
    obs_mean = jnp.mean(window_obs, axis=0)
    obs_anom = window_obs - obs_mean
    values = window_values(obs_values[batch_no])
    weights = window_values(obs_weights[batch_no])
    innov = weights * (values - obs_mean) - 0.5 * weights * obs_anom
    return (obs_anom, innov)


def observe_members(ensemble, obs_cell, op_select, op_table, batch_no):
    blocks = ensemble.reshape(ensemble.shape[0], ensemble.shape[1] // BLK, BLK)
    picked = blocks[:, obs_cell[batch_no, 0]]
    operators = op_table[op_select[batch_no, 0]]
    observed = jnp.einsum("koc,opc->kop", picked, operators, precision=lax.Precision.HIGHEST)
    observed = observed.reshape(ensemble.shape[0], OB * BLK)
    return lax.all_gather(observed, "member", axis=0, tiled=True)


def observe_owners(cells, obs_cell, op_select, op_table, batch_no):
    member_index = lax.axis_index("member")
    cell_index = obs_cell[batch_no, 0]
    owned = cell_index // CB_DEV == member_index
    local_idx = cell_index % CB_DEV
    blocks = cells.reshape(K, CB_DEV, BLK)
    picked = blocks[:, local_idx]
    operators = op_table[op_select[batch_no, 0]]
    observed = jnp.einsum("koc,opc->kop", picked, operators, precision=lax.Precision.HIGHEST)
    observed = observed * owned.astype(jnp.float32)[None, :, None]
    return lax.psum(observed.reshape(K, OB * BLK), "member")


def to_cells(ensemble):
    return lax.all_to_all(ensemble, "member", split_axis=1, concat_axis=0, tiled=True)


def to_members(cells):
    return lax.all_to_all(cells, "member", split_axis=0, concat_axis=1, tiled=True)


def update_cells(cells, obs_anom, innov, loc_obs, loc_tile, loc_tiles, batch_no):
    blocks = cells.reshape(K, CB_DEV, BLK)
    state_mean = jnp.mean(blocks, axis=0)
    anom_win = obs_anom.reshape(K, 3 * OB, BLK)
    innov_win = innov.reshape(K, 3 * OB, BLK)

    def update_block(packed):
        cell_blk, mean_blk, reach, tile_pick = packed
        state_anom = cell_blk - mean_blk
        chosen = anom_win[:, reach]
        covariance = jnp.einsum(
            "kc,klo->lco", state_anom, chosen, precision=lax.Precision.HIGHEST
        ) / (K - 1)
        gain = loc_tiles[tile_pick] * covariance
        increment = jnp.einsum(
            "klo,lco->kc", innov_win[:, reach], gain, precision=lax.Precision.HIGHEST
        )
        return cell_blk + increment

    fresh = lax.map(
        update_block,
        (blocks.transpose(1, 0, 2), state_mean, loc_obs[batch_no, 0], loc_tile[batch_no, 0]),
    )
    return fresh.transpose(1, 0, 2).reshape(K, CB_DEV * BLK)


def per_device(
    states, obs_values, obs_weights, obs_cell, op_select, op_table, loc_obs, loc_tile, loc_tiles
):
    ensemble = states
    window_obs = window(observe_members(ensemble, obs_cell, op_select, op_table, 0))
    obs_anom, innov = prepare(window_obs, obs_values, obs_weights, 0)
    cells = to_cells(ensemble)
    cells = update_cells(cells, obs_anom, innov, loc_obs, loc_tile, loc_tiles, 0)
    window_obs = window(observe_owners(cells, obs_cell, op_select, op_table, 1))
    obs_anom, innov = prepare(window_obs, obs_values, obs_weights, 1)
    cells = update_cells(cells, obs_anom, innov, loc_obs, loc_tile, loc_tiles, 1)
    ensemble = to_members(cells)
    return ensemble


def solution(mesh):
    placed = (
        P("member", "space"),
        P(),
        P(),
        P(None, "space", None),
        P(None, "space", None),
        P(),
        P(None, "space", "member", None),
        P(None, "space", "member", None),
        P(),
    )
    return jax.shard_map(
        per_device, mesh=mesh, in_specs=placed, out_specs=P("member", "space"), check_vma=False
    )
```

profile of v0, /device:TPU:0, one launch (start us, length us, event | category | flops | bytes accessed | tf_op | source)
XLA Modules:
  0.0 793.8 jit_solution(15951240218992025015)
XLA Ops:
  18.9 7.3 all-to-all-start
  26.2 88.9 %all-gather.2.cloned.1.call-done = f32[1024,512]{0,1:T(8,128)} async-done(((f32[128,512]{0,1:T(8,128)}), f32[1024,512]{0,1:T(8,128)}) %all-gather.2.cloned.1.call-update) | async-done | bytes 2097168 | tf_op jit(solution)/shard_map/all_gather | solution.py:55
  134.5 27.0 %collective-permute-done = f32[1024,512]{0,1:T(8,128)} collective-permute-done((f32[1024,512]{0,1:T(8,128)}, f32[1024,512]{0,1:T(8,128)}, u32[]{:S(2)}, u32[]{:S(2)}) %collective-permute-start) | collective-permute-done | bytes 2097184 | tf_op jit(solution)/shard_map/ppermute | solution.py:19
  164.9 6.6 multiply_subtract_fusion.1
  171.5 6.5 copy.82
  178.1 6.6 copy.83
  186.5 169.5 %while.20 = (s32[]{:T(128)}, f32[6,1024,128]{2,1,0:T(8,128)}, f32[6,1024,128]{1,2,0:T(8,128)}, s32[6,8]{1,0:T(8,128)S(1)}, f32[1024,12,128]{2,0,1:T(8,128)}, /*i...) while((s32[]{:T(128)}, f32[6,1024,128]{2,1,0:T(8,128)}, ...), condition=%wide.region_3.4_spmd, body=%wide.region_2.3_spmd.sunk | while | flops 3221751808 | bytes 32516496 | solution.py:98
  186.5 5.6 gather_fusion.1
  194.3 8.5 %fusion.107 = f32[8,128,128]{1,2,0:T(8,128)S(1)} fusion(f32[8,128,128]{1,2,0:T(8,128)S(1)} %copy.108, f32[8,1024,128]{2,1,0:T(8,128)} %gather_fusion.1, f32[1,1024,128]{2,1,0:T(8,128)S(1)} %copy.109, f32[128]{0:T(128)S(1)} %fusion.106), kind=kOutput, calls=%fused_computation.20.clone.1 | convolution fusion | flops 1611005952 | bytes 5767680 | tf_op jit(solution)/shard_map/while/body/eval_jaxpr/kc,klo->lco/dot_general | solution.py:89
  202.7 5.6 gather_fusion.2
  208.4 6.4 fusion.108
  214.8 5.6 gather_fusion.1
  222.5 8.5 %fusion.107 = f32[8,128,128]{1,2,0:T(8,128)S(1)} fusion(f32[8,128,128]{1,2,0:T(8,128)S(1)} %copy.108, f32[8,1024,128]{2,1,0:T(8,128)} %gather_fusion.1, f32[1,1024,128]{2,1,0:T(8,128)S(1)} %copy.109, f32[128]{0:T(128)S(1)} %fusion.106), kind=kOutput, calls=%fused_computation.20.clone.1 | convolution fusion | flops 1611005952 | bytes 5767680 | tf_op jit(solution)/shard_map/while/body/eval_jaxpr/kc,klo->lco/dot_general | solution.py:89
  231.0 5.6 gather_fusion.2
  236.6 6.4 fusion.108
  243.0 5.6 gather_fusion.1
  250.8 8.5 %fusion.107 = f32[8,128,128]{1,2,0:T(8,128)S(1)} fusion(f32[8,128,128]{1,2,0:T(8,128)S(1)} %copy.108, f32[8,1024,128]{2,1,0:T(8,128)} %gather_fusion.1, f32[1,1024,128]{2,1,0:T(8,128)S(1)} %copy.109, f32[128]{0:T(128)S(1)} %fusion.106), kind=kOutput, calls=%fused_computation.20.clone.1 | convolution fusion | flops 1611005952 | bytes 5767680 | tf_op jit(solution)/shard_map/while/body/eval_jaxpr/kc,klo->lco/dot_general | solution.py:89
  259.2 5.6 gather_fusion.2
  264.9 6.4 fusion.108
  271.3 5.6 gather_fusion.1
  279.0 8.5 %fusion.107 = f32[8,128,128]{1,2,0:T(8,128)S(1)} fusion(f32[8,128,128]{1,2,0:T(8,128)S(1)} %copy.108, f32[8,1024,128]{2,1,0:T(8,128)} %gather_fusion.1, f32[1,1024,128]{2,1,0:T(8,128)S(1)} %copy.109, f32[128]{0:T(128)S(1)} %fusion.106), kind=kOutput, calls=%fused_computation.20.clone.1 | convolution fusion | flops 1611005952 | bytes 5767680 | tf_op jit(solution)/shard_map/while/body/eval_jaxpr/kc,klo->lco/dot_general | solution.py:89
  287.5 5.6 gather_fusion.2
  293.1 6.4 fusion.108
  307.3 8.5 %fusion.107 = f32[8,128,128]{1,2,0:T(8,128)S(1)} fusion(f32[8,128,128]{1,2,0:T(8,128)S(1)} %copy.108, f32[8,1024,128]{2,1,0:T(8,128)} %gather_fusion.1, f32[1,1024,128]{2,1,0:T(8,128)S(1)} %copy.109, f32[128]{0:T(128)S(1)} %fusion.106), kind=kOutput, calls=%fused_computation.20.clone.1 | convolution fusion | flops 1611005952 | bytes 5767680 | tf_op jit(solution)/shard_map/while/body/eval_jaxpr/kc,klo->lco/dot_general | solution.py:89
  315.8 5.6 gather_fusion.2
  321.4 6.4 fusion.108
  335.5 8.5 %fusion.107 = f32[8,128,128]{1,2,0:T(8,128)S(1)} fusion(f32[8,128,128]{1,2,0:T(8,128)S(1)} %copy.108, f32[8,1024,128]{2,1,0:T(8,128)} %gather_fusion.1, f32[1,1024,128]{2,1,0:T(8,128)S(1)} %copy.109, f32[128]{0:T(128)S(1)} %fusion.106), kind=kOutput, calls=%fused_computation.20.clone.1 | convolution fusion | flops 1611005952 | bytes 5767680 | tf_op jit(solution)/shard_map/while/body/eval_jaxpr/kc,klo->lco/dot_general | solution.py:89
  344.0 5.6 gather_fusion.2
  349.6 6.4 fusion.108
  364.8 102.8 %all-reduce.2.cloned.1.call-done = f32[1024,512]{0,1:T(8,128)} async-done(((f32[1024,512]{0,1:T(8,128)}), f32[1024,512]{0,1:T(8,128)}) %all-reduce.2.cloned.1.call-update) | async-done | bytes 2097168 | tf_op jit(solution)/shard_map/psum | solution.py:68
  472.8 41.3 %collective-permute-done.2 = f32[1024,512]{0,1:T(8,128)} collective-permute-done((f32[1024,512]{0,1:T(8,128)}, f32[1024,512]{0,1:T(8,128)}, u32[]{:S(2)}, u32[]{:S(2)}) %collective-permute-start.2) | collective-permute-done | bytes 2097184 | tf_op jit(solution)/shard_map/ppermute | solution.py:19
  517.4 6.6 multiply_subtract_fusion
  524.0 6.6 copy.86
  530.6 6.5 copy.87
  539.0 162.1 %while.21 = (s32[]{:T(128)}, f32[6,1024,128]{2,1,0:T(8,128)}, f32[6,1024,128]{2,1,0:T(8,128)}, s32[6,8]{1,0:T(8,128)S(1)}, f32[1024,12,128]{2,0,1:T(8,128)}, /*i...) while((s32[]{:T(128)}, f32[6,1024,128]{2,1,0:T(8,128)}, ...), condition=%wide.region_8.9_spmd, body=%wide.region_7.8_spmd.sunk | while | flops 3221751808 | bytes 30419852 | solution.py:98
  545.4 8.6 %fusion.115 = f32[8,128,128]{1,2,0:T(8,128)S(1)} fusion(f32[8,128,128]{1,2,0:T(8,128)S(1)} %copy.110, f32[8,1024,128]{2,1,0:T(8,128)} %gather_fusion.4, f32[6,1024,128]{2,1,0:T(8,128)} %get-tuple-element.404, s32[]{:T(128)} %get-tuple-element.392, f32[128]{0:T(128)S(1)} %fusion.114), kind=kOutput, calls=%fused_computation.47.clone.1 | convolution fusion | flops 1611005952 | bytes 5768192 | tf_op jit(solution)/shard_map/while/body/eval_jaxpr/kc,klo->lco/dot_general | solution.py:89
  559.5 6.5 fusion.116
  572.4 8.6 %fusion.115 = f32[8,128,128]{1,2,0:T(8,128)S(1)} fusion(f32[8,128,128]{1,2,0:T(8,128)S(1)} %copy.110, f32[8,1024,128]{2,1,0:T(8,128)} %gather_fusion.4, f32[6,1024,128]{2,1,0:T(8,128)} %get-tuple-element.404, s32[]{:T(128)} %get-tuple-element.392, f32[128]{0:T(128)S(1)} %fusion.114), kind=kOutput, calls=%fused_computation.47.clone.1 | convolution fusion | flops 1611005952 | bytes 5768192 | tf_op jit(solution)/shard_map/while/body/eval_jaxpr/kc,klo->lco/dot_general | solution.py:89
  586.5 6.5 fusion.116
  599.4 8.6 %fusion.115 = f32[8,128,128]{1,2,0:T(8,128)S(1)} fusion(f32[8,128,128]{1,2,0:T(8,128)S(1)} %copy.110, f32[8,1024,128]{2,1,0:T(8,128)} %gather_fusion.4, f32[6,1024,128]{2,1,0:T(8,128)} %get-tuple-element.404, s32[]{:T(128)} %get-tuple-element.392, f32[128]{0:T(128)S(1)} %fusion.114), kind=kOutput, calls=%fused_computation.47.clone.1 | convolution fusion | flops 1611005952 | bytes 5768192 | tf_op jit(solution)/shard_map/while/body/eval_jaxpr/kc,klo->lco/dot_general | solution.py:89
  613.5 6.5 fusion.116
  626.4 8.6 %fusion.115 = f32[8,128,128]{1,2,0:T(8,128)S(1)} fusion(f32[8,128,128]{1,2,0:T(8,128)S(1)} %copy.110, f32[8,1024,128]{2,1,0:T(8,128)} %gather_fusion.4, f32[6,1024,128]{2,1,0:T(8,128)} %get-tuple-element.404, s32[]{:T(128)} %get-tuple-element.392, f32[128]{0:T(128)S(1)} %fusion.114), kind=kOutput, calls=%fused_computation.47.clone.1 | convolution fusion | flops 1611005952 | bytes 5768192 | tf_op jit(solution)/shard_map/while/body/eval_jaxpr/kc,klo->lco/dot_general | solution.py:89
  640.5 6.5 fusion.116
  653.4 8.6 %fusion.115 = f32[8,128,128]{1,2,0:T(8,128)S(1)} fusion(f32[8,128,128]{1,2,0:T(8,128)S(1)} %copy.110, f32[8,1024,128]{2,1,0:T(8,128)} %gather_fusion.4, f32[6,1024,128]{2,1,0:T(8,128)} %get-tuple-element.404, s32[]{:T(128)} %get-tuple-element.392, f32[128]{0:T(128)S(1)} %fusion.114), kind=kOutput, calls=%fused_computation.47.clone.1 | convolution fusion | flops 1611005952 | bytes 5768192 | tf_op jit(solution)/shard_map/while/body/eval_jaxpr/kc,klo->lco/dot_general | solution.py:89
  667.5 6.5 fusion.116
  680.4 8.6 %fusion.115 = f32[8,128,128]{1,2,0:T(8,128)S(1)} fusion(f32[8,128,128]{1,2,0:T(8,128)S(1)} %copy.110, f32[8,1024,128]{2,1,0:T(8,128)} %gather_fusion.4, f32[6,1024,128]{2,1,0:T(8,128)} %get-tuple-element.404, s32[]{:T(128)} %get-tuple-element.392, f32[128]{0:T(128)S(1)} %fusion.114), kind=kOutput, calls=%fused_computation.47.clone.1 | convolution fusion | flops 1611005952 | bytes 5768192 | tf_op jit(solution)/shard_map/while/body/eval_jaxpr/kc,klo->lco/dot_general | solution.py:89
  694.6 6.5 fusion.116
  707.9 75.6 %all_to_all.35 = f32[8,128,768]{1,2,0:T(8,128)} all-to-all(f32[8,128,768]{1,2,0:T(8,128)S(1)} %copy.89), channel_id=1, replica_groups=mesh['member'=8,'space'=4] {'member'}, dimensions={0} | all-to-all | bytes 6291456 | tf_op jit(solution)/shard_map/all_to_all | solution.py:76
  (181 shorter events, 161.1 us)
Async XLA Ops:
  6.5 10.3 %copy-start = (f32[8,128,128]{2,1,0:T(8,128)S(1)}, f32[8,128,128]{2,1,0:T(8,128)}, u32[]{:S(2)}) copy-start(f32[8,128,128]{2,1,0:T(8,128)} %param.18) | copy-start | bytes 1572868
  6.5 108.6 %all-gather.2.cloned.1.call-start = ((), (), s32[]{:S(2)}) async-start(), calls=%async_computation.2 | async-start | bytes 2359296 | tf_op jit(solution)/shard_map/all_gather | solution.py:55
  10.8 3.5 copy-start.9
  14.4 102.5 %copy-start.5 = (f32[2,2048]{1,0:T(2,128)S(1)}, f32[2,2048]{1,0:T(2,128)}, u32[]{:S(2)}) copy-start(f32[2,2048]{1,0:T(2,128)} %param.14) | copy-start | bytes 49156
  14.4 102.5 %copy-start.6 = (f32[2,2048]{1,0:T(2,128)S(1)}, f32[2,2048]{1,0:T(2,128)}, u32[]{:S(2)}) copy-start(f32[2,2048]{1,0:T(2,128)} %param.15) | copy-start | bytes 49156
  17.5 101.3 %copy-start.10 = (s32[2,1,4]{2,1,0:T(1,128)S(1)}, s32[2,1,4]{2,1,0:T(1,128)}, u32[]{:S(2)}) copy-start(s32[2,1,4]{2,1,0:T(1,128)} %param.16) | copy-start | bytes 100
  17.5 101.3 %copy-start.7 = (s32[2,1,6,8]{3,1,2,0:T(1,128)S(1)}, s32[2,1,6,8]{3,1,2,0:T(1,128)}, u32[]{:S(2)}) copy-start(s32[2,1,6,8]{3,1,2,0:T(1,128)} %param.20) | copy-start | bytes 1156
  17.5 101.3 %copy-start.8 = (s32[2,1,6,8]{3,1,2,0:T(1,128)S(1)}, s32[2,1,6,8]{3,1,2,0:T(1,128)}, u32[]{:S(2)}) copy-start(s32[2,1,6,8]{3,1,2,0:T(1,128)} %param.19) | copy-start | bytes 1156
  18.9 103.4 %all-to-all-start = ((f32[128,8,768]{0,2,1:T(8,128)}), f32[128,8,768]{0,2,1:T(8,128)}, u32[]{:S(2)}, u32[]{:S(2)}) async-start(f32[128,8,768]{0,2,1:T(8,128)} %bitcast.261), calls=%async_computation | async-start | bytes 6291456 | tf_op jit(solution)/shard_map/all_to_all | solution.py:72
  26.2 441.4 %all-reduce.2.cloned.1.call-start = ((), (), s32[]{:S(2)}) async-start(), calls=%async_computation.3 | async-start | bytes 4194304 | tf_op jit(solution)/shard_map/psum | solution.py:68
  115.1 46.4 %collective-permute-start = (f32[1024,512]{0,1:T(8,128)}, f32[1024,512]{0,1:T(8,128)}, u32[]{:S(2)}, u32[]{:S(2)}) collective-permute-start(f32[1024,512]{0,1:T(8,128)} %all-gather.2.cloned.1.call-done), channel_id=1, source_target_pairs={{0,1},{1,2},{2,3},{3,0},{4,5},{5,6},{6,7},{7,4},{8,9},{9,10},{10,1... | collective-permute-start | bytes 6291464 | tf_op jit(solution)/shard_map/ppermute | solution.py:19
  115.1 47.3 %collective-permute-start.1 = (f32[1024,512]{0,1:T(8,128)}, f32[1024,512]{0,1:T(8,128)}, u32[]{:S(2)}, u32[]{:S(2)}) collective-permute-start(f32[1024,512]{0,1:T(8,128)} %all-gather.2.cloned.1.call-done), channel_id=1, source_target_pairs={{1,0},{2,1},{3,2},{0,3},{5,4},{6,5},{7,6},{4,7},{9,8},{10,9},{11,1... | collective-permute-start | bytes 6291464 | tf_op jit(solution)/shard_map/ppermute | solution.py:21
  127.7 34.7 %copy-start.3 = (f32[1024,512]{0,1:T(8,128)S(1)}, f32[1024,512]{0,1:T(8,128)}, u32[]{:S(2)}) copy-start(f32[1024,512]{0,1:T(8,128)} %all-gather.2.cloned.1.call-done) | copy-start | bytes 6291460
  178.1 8.4 %copy-start.2 = (f32[8,128,128]{2,1,0:T(8,128)S(1)}, f32[8,128,128]{2,1,0:T(8,128)}, u32[]{:S(2)}) copy-start(f32[8,128,128]{2,1,0:T(8,128)} %param.21) | copy-start | bytes 1572868
  467.6 46.5 %collective-permute-start.2 = (f32[1024,512]{0,1:T(8,128)}, f32[1024,512]{0,1:T(8,128)}, u32[]{:S(2)}, u32[]{:S(2)}) collective-permute-start(f32[1024,512]{0,1:T(8,128)} %all-reduce.2.cloned.1.call-done), channel_id=1, source_target_pairs={{0,1},{1,2},{2,3},{3,0},{4,5},{5,6},{6,7},{7,4},{8,9},{9,10},{10,1... | collective-permute-start | bytes 6291464 | tf_op jit(solution)/shard_map/ppermute | solution.py:19
  467.6 47.2 %collective-permute-start.3 = (f32[1024,512]{0,1:T(8,128)}, f32[1024,512]{0,1:T(8,128)}, u32[]{:S(2)}, u32[]{:S(2)}) collective-permute-start(f32[1024,512]{0,1:T(8,128)} %all-reduce.2.cloned.1.call-done), channel_id=1, source_target_pairs={{1,0},{2,1},{3,2},{0,3},{5,4},{6,5},{7,6},{4,7},{9,8},{10,9},{11,1... | collective-permute-start | bytes 6291464 | tf_op jit(solution)/shard_map/ppermute | solution.py:21
  470.5 44.3 %copy-start.4 = (f32[1024,512]{0,1:T(8,128)S(1)}, f32[1024,512]{0,1:T(8,128)}, u32[]{:S(2)}) copy-start(f32[1024,512]{0,1:T(8,128)} %all-reduce.2.cloned.1.call-done) | copy-start | bytes 6291460
  707.8 79.1 %copy-start.1 = (f32[8,128,128]{2,1,0:T(8,128)S(1)}, f32[8,128,128]{2,1,0:T(8,128)}, u32[]{:S(2)}) copy-start(f32[8,128,128]{2,1,0:T(8,128)} %param.18) | copy-start | bytes 1572868
Sparse Core Ops, SparseCore 0:
  19.0 96.0 all-gather.1
  364.9 102.6 all-reduce.1
where the time goes:
time: 796 us; the launch traced here: 794 us
  waiting for transfers between devices  265 us (33%)
  local copies, waits for them, and re-layouts  219 us (28%)
  matrix products  186 us (23%)
  blocking collectives  75.6 us (9%)
  other arithmetic  23.5 us (3%)
  between operations  13.7 us (2%)
  starting transfers between devices  10.8 us (1%)
    psum x1, waiting for transfers between devices, observe_owners(): return lax.psum(observed.reshape(K, OB * BLK), 'member')  103 us
    dot_general x12, matrix products, update_block(): jnp.einsum('kc,klo->lco', state_anom, chosen, precision=lax.Precision.HIG...  102 us
    all_gather x1, waiting for transfers between devices, observe_members(): return lax.all_gather(observed, 'member', axis=0, tiled=True)  88.9 us
    dot_general x12, matrix products, update_block(): jnp.einsum('klo,lco->kc', innov_win[:, reach], gain, precision=lax.Precis...  77.6 us
    all_to_all x1, blocking collectives, to_members(): lax.all_to_all(cells, 'member', split_axis=0, concat_axis=1, tiled=True)  75.6 us
    ppermute x2, waiting for transfers between devices, with_halo(): lax.ppermute(tail, axis, [(i, (i + 1) % count) for i in range(count)])  68.4 us
    gather x12, local copies, waits for them, and re-layouts, update_block(): innov_win[:, reach]  67 us
    gather x12, local copies, waits for them, and re-layouts, update_block(): chosen = anom_win[:, reach]  67 us
  transfers between devices with their start and end apart: 7, of which 7 were waited for; matrix products, arithmetic and copies ran while one was open for 2% of the time, Pallas kernels for 0%

commit v1 on v0

--- a/solution.py
+++ b/solution.py
@@ -7,6 +7,13 @@
 BLK = 128
 CB_DEV = 6
 OB = 4
+
+
+def swapped_in(x, axis, along):
+    size = lax.axis_size(axis)
+    blocks = jnp.stack([x for _ in range(size)])
+    blocks = lax.all_to_all(blocks, axis, split_axis=0, concat_axis=0)
+    return jnp.concatenate(blocks, axis=along)
 
 
 def with_halo(cells, sides, width):
@@ -52,7 +59,7 @@
     operators = op_table[op_select[batch_no, 0]]
     observed = jnp.einsum("koc,opc->kop", picked, operators, precision=lax.Precision.HIGHEST)
     observed = observed.reshape(ensemble.shape[0], OB * BLK)
-    return lax.all_gather(observed, "member", axis=0, tiled=True)
+    return swapped_in(observed, "member", 0)
 
 
 def observe_owners(cells, obs_cell, op_select, op_table, batch_no):

time: 796 us -> 792 us (level)
  waiting for transfers between devices: 265 us -> 204 us
  blocking collectives: 75.6 us -> 131 us
    all_gather x1 -> x0, waiting for transfers between devices: 88.9 us -> none  [observe_members(): return lax.all_gather(observed, 'member', axis=0, tiled=True)]
    all_to_all x1, waiting for transfers between devices: 3.47 us -> 60.1 us  [to_cells(): lax.all_to_all(ensemble, 'member', split_axis=1, concat_axis=0, tiled=True)]
    all_to_all x0 -> x1, blocking collectives: none -> 55.3 us  [swapped_in(): blocks = lax.all_to_all(blocks, axis, split_axis=0, concat_axis=0)]
    ppermute x2, waiting for transfers between devices: 68.4 us -> 41.3 us  [with_halo(): lax.ppermute(tail, axis, [(i, (i + 1) % count) for i in range(count)])]
  transfers between devices with their start and end apart: 7 -> 6, of which waited for: 7 -> 4; matrix products, arithmetic and copies ran while one was open for 2% -> 3% of each run, Pallas kernels for 0% -> 0%
where the time goes in v1:
time: 792 us; the launch traced here: 789 us
  local copies, waits for them, and re-layouts  223 us (28%)
  waiting for transfers between devices  204 us (26%)
  matrix products  185 us (23%)
  blocking collectives  131 us (17%)
  other arithmetic  24.1 us (3%)
  between operations  13.7 us (2%)
  starting transfers between devices  8.11 us (1%)
    dot_general x12, matrix products, update_block(): jnp.einsum('kc,klo->lco', state_anom, chosen, precision=lax.Precision.HIG...  102 us
    psum x1, waiting for transfers between devices, observe_owners(): return lax.psum(observed.reshape(K, OB * BLK), 'member')  102 us
    dot_general x12, matrix products, update_block(): jnp.einsum('klo,lco->kc', innov_win[:, reach], gain, precision=lax.Precis...  77.6 us
    all_to_all x1, blocking collectives, to_members(): lax.all_to_all(cells, 'member', split_axis=0, concat_axis=1, tiled=True)  75.6 us
    gather x12, local copies, waits for them, and re-layouts, update_block(): innov_win[:, reach]  66.3 us
    gather x12, local copies, waits for them, and re-layouts, update_block(): chosen = anom_win[:, reach]  66.3 us
    all_to_all x1, waiting for transfers between devices, to_cells(): lax.all_to_all(ensemble, 'member', split_axis=1, concat_axis=0, tiled=True)  60.1 us
    all_to_all x1, blocking collectives, swapped_in(): blocks = lax.all_to_all(blocks, axis, split_axis=0, concat_axis=0)  55.3 us
  transfers between devices with their start and end apart: 6, of which 4 were waited for; matrix products, arithmetic and copies ran while one was open for 3% of the time, Pallas kernels for 0%

profile of v1, /device:TPU:0, one launch (start us, length us, event | category | flops | bytes accessed | tf_op | source)
XLA Modules:
  0.0 789.3 jit_solution(3340478874945987645)
XLA Ops:
  18.2 55.3 %all_to_all.40 = f32[8,128,512]{1,2,0:T(8,128)S(1)} all-to-all(f32[8,128,512]{1,2,0:T(8,128)S(1)} %stack.3), channel_id=1, replica_groups=mesh['member'=8,'space'=4] {'member'}, dimensions={0} | all-to-all | bytes 4194304 | tf_op jit(solution)/shard_map/all_to_all | solution.py:15
  87.9 60.1 %all-to-all-done = f32[128,8,768]{0,2,1:T(8,128)} async-done(((f32[128,8,768]{0,2,1:T(8,128)}), f32[128,8,768]{0,2,1:T(8,128)}, u32[]{:S(2)}, u32[]{:S(2)}) %all-to-all-start) | async-done | bytes 3145760 | tf_op jit(solution)/shard_map/all_to_all | solution.py:79
  163.1 6.6 multiply_subtract_fusion.1
  169.7 6.6 copy.83
  176.3 6.6 copy.84
  184.8 168.4 %while.20 = (s32[]{:T(128)}, f32[6,1024,128]{2,1,0:T(8,128)}, f32[6,1024,128]{1,2,0:T(8,128)}, s32[6,8]{1,0:T(8,128)S(1)}, f32[1024,12,128]{2,0,1:T(8,128)}, /*i...) while((s32[]{:T(128)}, f32[6,1024,128]{2,1,0:T(8,128)}, ...), condition=%wide.region_3.4_spmd, body=%wide.region_2.3_spmd.sunk | while | flops 3221751808 | bytes 32516496 | solution.py:105
  184.8 5.5 gather_fusion.1
  192.4 8.5 %fusion.108 = f32[8,128,128]{1,2,0:T(8,128)S(1)} fusion(f32[8,128,128]{1,2,0:T(8,128)S(1)} %copy.111, f32[8,1024,128]{2,1,0:T(8,128)} %gather_fusion.1, f32[1,1024,128]{2,1,0:T(8,128)S(1)} %copy.112, f32[128]{0:T(128)S(1)} %fusion.107), kind=kOutput, calls=%fused_computation.20.clone.1 | convolution fusion | flops 1611005952 | bytes 5767680 | tf_op jit(solution)/shard_map/while/body/eval_jaxpr/kc,klo->lco/dot_general | solution.py:96
  200.9 5.5 gather_fusion.2
  206.4 6.4 fusion.109
  220.5 8.5 %fusion.108 = f32[8,128,128]{1,2,0:T(8,128)S(1)} fusion(f32[8,128,128]{1,2,0:T(8,128)S(1)} %copy.111, f32[8,1024,128]{2,1,0:T(8,128)} %gather_fusion.1, f32[1,1024,128]{2,1,0:T(8,128)S(1)} %copy.112, f32[128]{0:T(128)S(1)} %fusion.107), kind=kOutput, calls=%fused_computation.20.clone.1 | convolution fusion | flops 1611005952 | bytes 5767680 | tf_op jit(solution)/shard_map/while/body/eval_jaxpr/kc,klo->lco/dot_general | solution.py:96
  229.0 5.5 gather_fusion.2
  234.5 6.4 fusion.109
  248.5 8.5 %fusion.108 = f32[8,128,128]{1,2,0:T(8,128)S(1)} fusion(f32[8,128,128]{1,2,0:T(8,128)S(1)} %copy.111, f32[8,1024,128]{2,1,0:T(8,128)} %gather_fusion.1, f32[1,1024,128]{2,1,0:T(8,128)S(1)} %copy.112, f32[128]{0:T(128)S(1)} %fusion.107), kind=kOutput, calls=%fused_computation.20.clone.1 | convolution fusion | flops 1611005952 | bytes 5767680 | tf_op jit(solution)/shard_map/while/body/eval_jaxpr/kc,klo->lco/dot_general | solution.py:96
  257.0 5.5 gather_fusion.2
  262.5 6.4 fusion.109
  276.6 8.5 %fusion.108 = f32[8,128,128]{1,2,0:T(8,128)S(1)} fusion(f32[8,128,128]{1,2,0:T(8,128)S(1)} %copy.111, f32[8,1024,128]{2,1,0:T(8,128)} %gather_fusion.1, f32[1,1024,128]{2,1,0:T(8,128)S(1)} %copy.112, f32[128]{0:T(128)S(1)} %fusion.107), kind=kOutput, calls=%fused_computation.20.clone.1 | convolution fusion | flops 1611005952 | bytes 5767680 | tf_op jit(solution)/shard_map/while/body/eval_jaxpr/kc,klo->lco/dot_general | solution.py:96
  285.1 5.5 gather_fusion.2
  290.6 6.4 fusion.109
  304.7 8.5 %fusion.108 = f32[8,128,128]{1,2,0:T(8,128)S(1)} fusion(f32[8,128,128]{1,2,0:T(8,128)S(1)} %copy.111, f32[8,1024,128]{2,1,0:T(8,128)} %gather_fusion.1, f32[1,1024,128]{2,1,0:T(8,128)S(1)} %copy.112, f32[128]{0:T(128)S(1)} %fusion.107), kind=kOutput, calls=%fused_computation.20.clone.1 | convolution fusion | flops 1611005952 | bytes 5767680 | tf_op jit(solution)/shard_map/while/body/eval_jaxpr/kc,klo->lco/dot_general | solution.py:96
  313.2 5.5 gather_fusion.2
  318.7 6.4 fusion.109
  332.7 8.5 %fusion.108 = f32[8,128,128]{1,2,0:T(8,128)S(1)} fusion(f32[8,128,128]{1,2,0:T(8,128)S(1)} %copy.111, f32[8,1024,128]{2,1,0:T(8,128)} %gather_fusion.1, f32[1,1024,128]{2,1,0:T(8,128)S(1)} %copy.112, f32[128]{0:T(128)S(1)} %fusion.107), kind=kOutput, calls=%fused_computation.20.clone.1 | convolution fusion | flops 1611005952 | bytes 5767680 | tf_op jit(solution)/shard_map/while/body/eval_jaxpr/kc,klo->lco/dot_general | solution.py:96
  341.2 5.5 gather_fusion.2
  346.7 6.5 fusion.109
  361.9 101.5 %all-reduce.2.cloned.1.call-done = f32[1024,512]{0,1:T(8,128)} async-done(((f32[1024,512]{0,1:T(8,128)}), f32[1024,512]{0,1:T(8,128)}) %all-reduce.2.cloned.1.call-update) | async-done | bytes 2097168 | tf_op jit(solution)/shard_map/psum | solution.py:75
  468.6 41.3 %collective-permute-done.2 = f32[1024,512]{0,1:T(8,128)} collective-permute-done((f32[1024,512]{0,1:T(8,128)}, f32[1024,512]{0,1:T(8,128)}, u32[]{:S(2)}, u32[]{:S(2)}) %collective-permute-start.2) | collective-permute-done | bytes 2097184 | tf_op jit(solution)/shard_map/ppermute | solution.py:26
  513.2 6.6 multiply_subtract_fusion
  519.7 6.6 copy.87
  526.3 6.6 copy.88
  534.7 161.8 %while.21 = (s32[]{:T(128)}, f32[6,1024,128]{2,1,0:T(8,128)}, f32[6,1024,128]{2,1,0:T(8,128)}, s32[6,8]{1,0:T(8,128)S(1)}, f32[1024,12,128]{2,0,1:T(8,128)}, /*i...) while((s32[]{:T(128)}, f32[6,1024,128]{2,1,0:T(8,128)}, ...), condition=%wide.region_8.9_spmd, body=%wide.region_7.8_spmd.sunk | while | flops 3221751808 | bytes 30419852 | solution.py:105
  541.1 8.6 %fusion.116 = f32[8,128,128]{1,2,0:T(8,128)S(1)} fusion(f32[8,128,128]{1,2,0:T(8,128)S(1)} %copy.113, f32[8,1024,128]{2,1,0:T(8,128)} %gather_fusion.4, f32[6,1024,128]{2,1,0:T(8,128)} %get-tuple-element.404, s32[]{:T(128)} %get-tuple-element.392, f32[128]{0:T(128)S(1)} %fusion.115), kind=kOutput, calls=%fused_computation.47.clone.1 | convolution fusion | flops 1611005952 | bytes 5768192 | tf_op jit(solution)/shard_map/while/body/eval_jaxpr/kc,klo->lco/dot_general | solution.py:96
  549.7 5.5 gather_fusion.5
  555.2 6.5 fusion.117
  568.1 8.6 %fusion.116 = f32[8,128,128]{1,2,0:T(8,128)S(1)} fusion(f32[8,128,128]{1,2,0:T(8,128)S(1)} %copy.113, f32[8,1024,128]{2,1,0:T(8,128)} %gather_fusion.4, f32[6,1024,128]{2,1,0:T(8,128)} %get-tuple-element.404, s32[]{:T(128)} %get-tuple-element.392, f32[128]{0:T(128)S(1)} %fusion.115), kind=kOutput, calls=%fused_computation.47.clone.1 | convolution fusion | flops 1611005952 | bytes 5768192 | tf_op jit(solution)/shard_map/while/body/eval_jaxpr/kc,klo->lco/dot_general | solution.py:96
  576.6 5.5 gather_fusion.5
  582.2 6.5 fusion.117
  595.0 8.6 %fusion.116 = f32[8,128,128]{1,2,0:T(8,128)S(1)} fusion(f32[8,128,128]{1,2,0:T(8,128)S(1)} %copy.113, f32[8,1024,128]{2,1,0:T(8,128)} %gather_fusion.4, f32[6,1024,128]{2,1,0:T(8,128)} %get-tuple-element.404, s32[]{:T(128)} %get-tuple-element.392, f32[128]{0:T(128)S(1)} %fusion.115), kind=kOutput, calls=%fused_computation.47.clone.1 | convolution fusion | flops 1611005952 | bytes 5768192 | tf_op jit(solution)/shard_map/while/body/eval_jaxpr/kc,klo->lco/dot_general | solution.py:96
  603.6 5.5 gather_fusion.5
  609.1 6.5 fusion.117
  622.0 8.6 %fusion.116 = f32[8,128,128]{1,2,0:T(8,128)S(1)} fusion(f32[8,128,128]{1,2,0:T(8,128)S(1)} %copy.113, f32[8,1024,128]{2,1,0:T(8,128)} %gather_fusion.4, f32[6,1024,128]{2,1,0:T(8,128)} %get-tuple-element.404, s32[]{:T(128)} %get-tuple-element.392, f32[128]{0:T(128)S(1)} %fusion.115), kind=kOutput, calls=%fused_computation.47.clone.1 | convolution fusion | flops 1611005952 | bytes 5768192 | tf_op jit(solution)/shard_map/while/body/eval_jaxpr/kc,klo->lco/dot_general | solution.py:96
  630.6 5.5 gather_fusion.5
  636.1 6.5 fusion.117
  649.0 8.6 %fusion.116 = f32[8,128,128]{1,2,0:T(8,128)S(1)} fusion(f32[8,128,128]{1,2,0:T(8,128)S(1)} %copy.113, f32[8,1024,128]{2,1,0:T(8,128)} %gather_fusion.4, f32[6,1024,128]{2,1,0:T(8,128)} %get-tuple-element.404, s32[]{:T(128)} %get-tuple-element.392, f32[128]{0:T(128)S(1)} %fusion.115), kind=kOutput, calls=%fused_computation.47.clone.1 | convolution fusion | flops 1611005952 | bytes 5768192 | tf_op jit(solution)/shard_map/while/body/eval_jaxpr/kc,klo->lco/dot_general | solution.py:96
  663.1 6.5 fusion.117
  676.0 8.6 %fusion.116 = f32[8,128,128]{1,2,0:T(8,128)S(1)} fusion(f32[8,128,128]{1,2,0:T(8,128)S(1)} %copy.113, f32[8,1024,128]{2,1,0:T(8,128)} %gather_fusion.4, f32[6,1024,128]{2,1,0:T(8,128)} %get-tuple-element.404, s32[]{:T(128)} %get-tuple-element.392, f32[128]{0:T(128)S(1)} %fusion.115), kind=kOutput, calls=%fused_computation.47.clone.1 | convolution fusion | flops 1611005952 | bytes 5768192 | tf_op jit(solution)/shard_map/while/body/eval_jaxpr/kc,klo->lco/dot_general | solution.py:96
  690.1 6.5 fusion.117
  703.4 75.6 %all_to_all.41 = f32[8,128,768]{1,2,0:T(8,128)} all-to-all(f32[8,128,768]{1,2,0:T(8,128)S(1)} %copy.90), channel_id=1, replica_groups=mesh['member'=8,'space'=4] {'member'}, dimensions={0} | all-to-all | bytes 6291456 | tf_op jit(solution)/shard_map/all_to_all | solution.py:83
  (181 shorter events, 161.2 us)
Async XLA Ops:
  6.5 10.3 %copy-start = (f32[8,128,128]{2,1,0:T(8,128)S(1)}, f32[8,128,128]{2,1,0:T(8,128)}, u32[]{:S(2)}) copy-start(f32[8,128,128]{2,1,0:T(8,128)} %param.18) | copy-start | bytes 1572868
  10.8 3.5 copy-start.8
  73.6 8.0 %copy-start.4 = (f32[2,2048]{1,0:T(2,128)S(1)}, f32[2,2048]{1,0:T(2,128)}, u32[]{:S(2)}) copy-start(f32[2,2048]{1,0:T(2,128)} %param.14) | copy-start | bytes 49156
  73.6 8.0 %copy-start.5 = (f32[2,2048]{1,0:T(2,128)S(1)}, f32[2,2048]{1,0:T(2,128)}, u32[]{:S(2)}) copy-start(f32[2,2048]{1,0:T(2,128)} %param.15) | copy-start | bytes 49156
  73.6 9.9 %copy-start.9 = (s32[2,1,4]{2,1,0:T(1,128)S(1)}, s32[2,1,4]{2,1,0:T(1,128)}, u32[]{:S(2)}) copy-start(s32[2,1,4]{2,1,0:T(1,128)} %param.16) | copy-start | bytes 100
  73.6 9.9 %copy-start.6 = (s32[2,1,6,8]{3,1,2,0:T(1,128)S(1)}, s32[2,1,6,8]{3,1,2,0:T(1,128)}, u32[]{:S(2)}) copy-start(s32[2,1,6,8]{3,1,2,0:T(1,128)} %param.20) | copy-start | bytes 1156
  73.6 10.0 %copy-start.7 = (s32[2,1,6,8]{3,1,2,0:T(1,128)S(1)}, s32[2,1,6,8]{3,1,2,0:T(1,128)}, u32[]{:S(2)}) copy-start(s32[2,1,6,8]{3,1,2,0:T(1,128)} %param.19) | copy-start | bytes 1156
  73.6 74.4 %all-to-all-start = ((f32[128,8,768]{0,2,1:T(8,128)}), f32[128,8,768]{0,2,1:T(8,128)}, u32[]{:S(2)}, u32[]{:S(2)}) async-start(f32[128,8,768]{0,2,1:T(8,128)} %bitcast.267), calls=%async_computation | async-start | bytes 6291456 | tf_op jit(solution)/shard_map/all_to_all | solution.py:79
  78.2 385.3 %all-reduce.2.cloned.1.call-start = ((), (), s32[]{:S(2)}) async-start(), calls=%async_computation.3 | async-start | bytes 4194304 | tf_op jit(solution)/shard_map/psum | solution.py:75
  79.8 80.2 %collective-permute-start = (f32[1024,512]{0,1:T(8,128)}, f32[1024,512]{0,1:T(8,128)}, u32[]{:S(2)}, u32[]{:S(2)}) collective-permute-start(f32[1024,512]{0,1:T(8,128)} %copy_bitcast_fusion), channel_id=1, source_target_pairs={{0,1},{1,2},{2,3},{3,0},{4,5},{5,6},{6,7},{7,4},{8,9},{9,10},{10,1... | collective-permute-start | bytes 6291464 | tf_op jit(solution)/shard_map/ppermute | solution.py:26
  79.8 80.2 %collective-permute-start.1 = (f32[1024,512]{0,1:T(8,128)}, f32[1024,512]{0,1:T(8,128)}, u32[]{:S(2)}, u32[]{:S(2)}) collective-permute-start(f32[1024,512]{0,1:T(8,128)} %copy_bitcast_fusion), channel_id=1, source_target_pairs={{1,0},{2,1},{3,2},{0,3},{5,4},{6,5},{7,6},{4,7},{9,8},{10,9},{11,1... | collective-permute-start | bytes 6291464 | tf_op jit(solution)/shard_map/ppermute | solution.py:28
  176.3 8.5 %copy-start.2 = (f32[8,128,128]{2,1,0:T(8,128)S(1)}, f32[8,128,128]{2,1,0:T(8,128)}, u32[]{:S(2)}) copy-start(f32[8,128,128]{2,1,0:T(8,128)} %param.21) | copy-start | bytes 1572868
  463.4 46.5 %collective-permute-start.2 = (f32[1024,512]{0,1:T(8,128)}, f32[1024,512]{0,1:T(8,128)}, u32[]{:S(2)}, u32[]{:S(2)}) collective-permute-start(f32[1024,512]{0,1:T(8,128)} %all-reduce.2.cloned.1.call-done), channel_id=1, source_target_pairs={{0,1},{1,2},{2,3},{3,0},{4,5},{5,6},{6,7},{7,4},{8,9},{9,10},{10,1... | collective-permute-start | bytes 6291464 | tf_op jit(solution)/shard_map/ppermute | solution.py:26
  463.4 47.2 %collective-permute-start.3 = (f32[1024,512]{0,1:T(8,128)}, f32[1024,512]{0,1:T(8,128)}, u32[]{:S(2)}, u32[]{:S(2)}) collective-permute-start(f32[1024,512]{0,1:T(8,128)} %all-reduce.2.cloned.1.call-done), channel_id=1, source_target_pairs={{1,0},{2,1},{3,2},{0,3},{5,4},{6,5},{7,6},{4,7},{9,8},{10,9},{11,1... | collective-permute-start | bytes 6291464 | tf_op jit(solution)/shard_map/ppermute | solution.py:28
  466.3 44.3 %copy-start.3 = (f32[1024,512]{0,1:T(8,128)S(1)}, f32[1024,512]{0,1:T(8,128)}, u32[]{:S(2)}) copy-start(f32[1024,512]{0,1:T(8,128)} %all-reduce.2.cloned.1.call-done) | copy-start | bytes 6291460
  703.3 79.1 %copy-start.1 = (f32[8,128,128]{2,1,0:T(8,128)S(1)}, f32[8,128,128]{2,1,0:T(8,128)}, u32[]{:S(2)}) copy-start(f32[8,128,128]{2,1,0:T(8,128)} %param.18) | copy-start | bytes 1572868
Sparse Core Ops, SparseCore 0:
  362.0 101.3 all-reduce.1
